TPU v7x, 32 devices: a whole 2x2x4 slice. The times are simulated.
32 devices in a mesh: ctx: 8 (over z, y), head: 4 (over x, core).
Axes of the slice: x: 2, y: 2, z: 4, core: 2. Of those that a mesh axis runs over, the one named last changes fastest.
Arguments:
- queries: bfloat16 [2048, 6144], P(('ctx', 'head')), may hold values from -42 to 42
- key_head_columns: bfloat16 [2048, 512], P(('ctx', 'head')), may hold values from -4 to 4
- value_head_columns: bfloat16 [2048, 512], P(('ctx', 'head')), may hold values from -6 to 6
- output_gradient: bfloat16 [2048, 6144], P(('ctx', 'head')), may hold values from -6 to 6
- file_starts: int32 [5], replicated, may hold values from 0 to 1984, as said below
- file_imports: int32 [5, 4], replicated, may hold values from -1 to 4, as said below
- header_lens: int32 [5], replicated, may hold values from 16 to 64
Outputs:
- grad_queries: float32 [2048, 6144], P(('ctx', 'head'))
- key_gradient: float32 [2048, 512], P(('ctx', 'head'))
- value_gradient: float32 [2048, 512], P(('ctx', 'head'))
Inputs may be any that keep to these rules, and one draw needn't show every extreme that they name: `file_starts`: Increasing; the first is 0 and the last is 1984; each is a multiple of 64; no two lie in the same aligned block of 256 tokens; each file has 64 tokens or more. `file_imports`: each row lists distinct files other than its own, then -1 in the unused places; file 0 imports nothing.
All inputs are finite; a program needn't handle non-finite values.
Results may differ from a plain program's by a relative error of at most 0.004.
Values may be sent and summed in bfloat16 or wider, within the bound.
No kernel may reach another device: no remote copies, remote signals or barrier semaphores. Data moves between devices by JAX's collectives and lax.ppermute only.
A program may use at most 64 MiB of HBM per device.

v0:
```python
import math
import jax
import jax.numpy as jnp
from jax import lax
from jax.sharding import PartitionSpec as P

WIN = 1024
HDR = 64


def passed_along(value, axis, steps):
    count = lax.axis_size(axis)
    first, last = (max(0, -steps), min(count, count - steps))
    return lax.ppermute(value, axis, [(source, source + steps) for source in range(first, last)])


def local_files(file_starts, file_imports, header_lens, offset_base, span_rows):
    places = offset_base + jnp.arange(span_rows, dtype=jnp.int32)
    before = file_starts[None, :] <= places[:, None]
    file_of = jnp.sum(before.astype(jnp.int32), axis=1) - 1
    file_begin = jnp.max(jnp.where(before, file_starts[None, :], 0), axis=1)
    lower_file = file_of[0]
    upper_file = file_of[span_rows - 1]
    per_file = file_imports.shape[1]
    lower_list = lax.dynamic_slice_in_dim(file_imports, lower_file, 1, 0)[0]
    upper_list = lax.dynamic_slice_in_dim(file_imports, upper_file, 1, 0)[0]
    targets = jnp.concatenate([lower_list, upper_list])
    source_file = jnp.concatenate(
        [jnp.full((per_file,), lower_file, jnp.int32), jnp.full((per_file,), upper_file, jnp.int32)]
    )
    usable = (targets >= 0) & (
        (jnp.arange(2 * per_file, dtype=jnp.int32) < per_file) | (upper_file != lower_file)
    )
    matches = jnp.arange(file_starts.shape[0], dtype=jnp.int32)[None, :] == targets[:, None]
    target_start = jnp.sum(jnp.where(matches, file_starts[None, :], 0), axis=1)
    target_len = jnp.sum(jnp.where(matches, header_lens[None, :], 0), axis=1)
    return (places, file_of, file_begin, source_file, usable, target_start, target_len)


def visibility(places, file_of, file_begin, key_places, source_file, usable, target_len):
    window_ok = (
        (key_places[None, :] <= places[:, None])
        & (key_places[None, :] > places[:, None] - WIN)
        & (key_places[None, :] >= file_begin[:, None])
    )
    offsets = jnp.arange(usable.shape[0] * HDR, dtype=jnp.int32) % HDR
    header_ok = jnp.repeat(usable, HDR) & (offsets < jnp.repeat(target_len, HDR))
    header_vis = header_ok[None, :] & (file_of[:, None] == jnp.repeat(source_file, HDR)[None, :])
    return jnp.concatenate([window_ok, header_vis], axis=1)


def per_device(
    queries,
    key_head_columns,
    value_head_columns,
    output_gradient,
    file_starts,
    file_imports,
    header_lens,
):
    query_rows, key_rows, value_rows, grad_rows = (
        lax.all_to_all(queries, "head", split_axis=1, concat_axis=0, tiled=True),
        lax.all_to_all(key_head_columns, "head", split_axis=1, concat_axis=0, tiled=True),
        lax.all_to_all(value_head_columns, "head", split_axis=1, concat_axis=0, tiled=True),
        lax.all_to_all(output_gradient, "head", split_axis=1, concat_axis=0, tiled=True),
    )
    tokens_here = key_rows.shape[0]
    head_size = key_rows.shape[1]
    queries_per_group = query_rows.shape[1] // head_size
    shard_index = lax.axis_index("ctx")
    offset_base = shard_index * tokens_here
    scaling = 1.0 / math.sqrt(head_size)
    reach = WIN // tokens_here
    places, file_of, file_begin, source_file, usable, target_start, target_len = local_files(
        file_starts, file_imports, header_lens, offset_base, tokens_here
    )
    block_count = source_file.shape[0]
    stacked = jnp.concatenate([key_rows, value_rows], axis=1)
    earlier = []
    for distance in range(1, reach + 1):
        earlier.append(passed_along(stacked, "ctx", distance))
    inside = (file_starts >= offset_base) & (file_starts < offset_base + tokens_here)
    own_offset = jnp.sum(jnp.where(inside, file_starts - offset_base, 0))
    own_header = lax.dynamic_slice_in_dim(stacked, own_offset, HDR, 0)
    all_headers = lax.all_gather(own_header, "ctx", axis=0, tiled=True)
    header_rows = jnp.concatenate(
        [
            lax.dynamic_slice_in_dim(all_headers, target_start[index] // tokens_here * HDR, HDR, 0)
            for index in range(block_count)
        ],
        axis=0,
    )
    key_table = jnp.concatenate(earlier[::-1] + [stacked, header_rows], axis=0)
    key_matrix = key_table[:, :head_size]
    value_matrix = key_table[:, head_size:]
    window_len = (reach + 1) * tokens_here
    key_places = offset_base - reach * tokens_here + jnp.arange(window_len, dtype=jnp.int32)
    visible = visibility(places, file_of, file_begin, key_places, source_file, usable, target_len)
    heads_block = max(
        (
            divisor
            for divisor in range(1, queries_per_group + 1)
            if queries_per_group % divisor == 0 and divisor * tokens_here <= max(512, tokens_here)
        )
    )
    block_total = queries_per_group // heads_block
    query_blocks = (
        query_rows.reshape(tokens_here, queries_per_group, head_size)
        .transpose(1, 0, 2)
        .reshape(block_total, heads_block, tokens_here, head_size)
    )
    grad_blocks = (
        grad_rows.reshape(tokens_here, queries_per_group, head_size)
        .transpose(1, 0, 2)
        .reshape(block_total, heads_block, tokens_here, head_size)
    )

    def attend(carry, inputs):
        key_gradient_sum, value_gradient_sum = carry
        query_block, grad_block = inputs
        scores = (
            jnp.einsum("htd,kd->htk", query_block, key_matrix, preferred_element_type=jnp.float32)
            * scaling
        )
        scores = jnp.where(visible[None], scores, -jnp.inf)
        ceiling = jnp.max(scores, axis=-1, keepdims=True)
        log_total = ceiling + jnp.log(jnp.sum(jnp.exp(scores - ceiling), axis=-1, keepdims=True))
        weights = jnp.exp(scores - log_total)
        grad_weights = jnp.einsum(
            "htd,kd->htk", grad_block, value_matrix, preferred_element_type=jnp.float32
        )
        centre = jnp.sum(weights * grad_weights, axis=-1, keepdims=True)
        grad_scores = (weights * (grad_weights - centre)).astype(jnp.bfloat16)
        weights_low = weights.astype(jnp.bfloat16)
        grad_query = (
            jnp.einsum("htk,kd->htd", grad_scores, key_matrix, preferred_element_type=jnp.float32)
            * scaling
        )
        key_gradient_sum = (
            key_gradient_sum
            + jnp.einsum(
                "htk,htd->kd", grad_scores, query_block, preferred_element_type=jnp.float32
            )
            * scaling
        )
        value_gradient_sum = value_gradient_sum + jnp.einsum(
            "htk,htd->kd", weights_low, grad_block, preferred_element_type=jnp.float32
        )
        return ((key_gradient_sum, value_gradient_sum), grad_query)

    empty_gradient = jnp.zeros((key_table.shape[0], head_size), jnp.float32)
    (key_gradient_sum, value_gradient_sum), grad_query = lax.scan(
        attend, (empty_gradient, empty_gradient), (query_blocks, grad_blocks)
    )
    grad_query = (
        grad_query.reshape(queries_per_group, tokens_here, head_size)
        .transpose(1, 0, 2)
        .reshape(tokens_here, queries_per_group * head_size)
    )
    combined = jnp.concatenate([key_gradient_sum, value_gradient_sum], axis=1)

    def window_part(index):
        return combined[index * tokens_here : (index + 1) * tokens_here]

    collected = window_part(reach)
    for distance in range(1, reach + 1):
        collected = collected + passed_along(window_part(reach - distance), "ctx", -distance)
    header_part = combined[window_len:]
    blocks_out = header_part.reshape(block_count, HDR, 2 * head_size)
    holders = jnp.where(usable, target_start // tokens_here, -1)
    block_piece = lax.all_gather(blocks_out, "ctx", axis=0, tiled=True)
    holder_piece = lax.all_gather(holders, "ctx", axis=0, tiled=True)
    selected = (holder_piece == shard_index).astype(jnp.float32)
    arriving = jnp.einsum("m,mrc->rc", selected, block_piece)
    current = lax.dynamic_slice_in_dim(collected, own_offset, HDR, 0)
    collected = lax.dynamic_update_slice_in_dim(collected, current + arriving, own_offset, 0)
    grad_queries, key_gradient, value_gradient = (
        lax.all_to_all(grad_query, "head", split_axis=0, concat_axis=1, tiled=True),
        lax.all_to_all(collected[:, :head_size], "head", split_axis=0, concat_axis=1, tiled=True),
        lax.all_to_all(collected[:, head_size:], "head", split_axis=0, concat_axis=1, tiled=True),
    )
    return (grad_queries, key_gradient, value_gradient)


def solution(mesh):
    in_specs = (
        P(("ctx", "head"), None),
        P(("ctx", "head"), None),
        P(("ctx", "head"), None),
        P(("ctx", "head"), None),
        P(),
        P(),
        P(),
    )
    out_specs = (P(("ctx", "head"), None), P(("ctx", "head"), None), P(("ctx", "head"), None))
    return jax.shard_map(
        per_device, mesh=mesh, in_specs=in_specs, out_specs=out_specs, check_vma=False
    )
```

profile of v0, /device:TPU:0, one launch (start us, length us, event | category | flops | bytes accessed | tf_op | source)
XLA Modules:
  0.0 296.5 jit_solution(10358402667834652991)
XLA Ops:
  8.7 4.2 %all-to-all-start.1 = ((bf16[64,4,128]{2,0,1:T(8,128)(2,1)}), bf16[64,4,128]{2,0,1:T(8,128)(2,1)S(1)}, u32[]{:S(2)}, u32[]{:S(2)}) async-start(bf16[64,4,128]{2,0,1:T(8,128)(2,1)} %copy_bitcast_fusion.6), calls=%async_computation.1 | async-start | bytes 131072 | tf_op jit(solution)/shard_map/all_to_all | solution.py:63
  18.2 1.5 copy_bitcast_fusion.5
  21.1 1.0 fusion.33
  23.0 1.3 dynamic-slice
  28.4 3.3 %all-to-all-start.2 = ((bf16[64,4,128]{2,0,1:T(8,128)(2,1)}), bf16[64,4,128]{2,0,1:T(8,128)(2,1)S(1)}, u32[]{:S(2)}, u32[]{:S(2)}) async-start(bf16[64,4,128]{2,0,1:T(8,128)(2,1)} %copy_bitcast_fusion.5), calls=%async_computation.2 | async-start | bytes 131072 | tf_op jit(solution)/shard_map/all_to_all | solution.py:64
  31.7 1.4 fusion.41
  55.0 1.0 copy.95
  55.9 1.0 copy.96
  57.7 3.5 %all-to-all-start.3 = ((bf16[64,4,1536]{2,0,1:T(8,128)(2,1)}), bf16[64,4,1536]{2,0,1:T(8,128)(2,1)S(1)}, u32[]{:S(2)}, u32[]{:S(2)}) async-start(bf16[64,4,1536]{2,0,1:T(8,128)(2,1)} %bitcast.142), calls=%async_computation.3 | async-start | bytes 1572864 | tf_op jit(solution)/shard_map/all_to_all | solution.py:65
  61.2 5.0 %collective-permute-start = (bf16[256,256]{1,0:T(8,128)(2,1)S(1)}, bf16[256,256]{1,0:T(8,128)(2,1)S(1)}, u32[]{:S(2)}, u32[]{:S(2)}) collective-permute-start(bf16[256,256]{1,0:T(8,128)(2,1)S(1)} %pad_maximum_fusion), channel_id=1, source_target_pairs={{0,16},{4,20},{8,24},{12,28},{1,17},{5,21},{9,25},{13,29},{2,18},{... | collective-permute-start | bytes 393224 | tf_op jit(solution)/shard_map/ppermute | solution.py:14
  66.2 4.4 %collective-permute-start.1 = (bf16[256,256]{1,0:T(8,128)(2,1)S(1)}, bf16[256,256]{1,0:T(8,128)(2,1)S(1)}, u32[]{:S(2)}, u32[]{:S(2)}) collective-permute-start(bf16[256,256]{1,0:T(8,128)(2,1)S(1)} %pad_maximum_fusion), channel_id=1, source_target_pairs={{0,12},{4,16},{8,20},{12,24},{16,28},{1,13},{5,17},{9,21},{13,25},... | collective-permute-start | bytes 393224 | tf_op jit(solution)/shard_map/ppermute | solution.py:14
  70.7 1.3 collective-permute-start.2
  72.0 3.1 %collective-permute-start.3 = (bf16[256,256]{1,0:T(8,128)(2,1)S(1)}, bf16[256,256]{1,0:T(8,128)(2,1)S(1)}, u32[]{:S(2)}, u32[]{:S(2)}) collective-permute-start(bf16[256,256]{1,0:T(8,128)(2,1)S(1)} %pad_maximum_fusion), channel_id=1, source_target_pairs={{0,4},{4,8},{8,12},{12,16},{16,20},{20,24},{24,28},{1,5},{5,9},{9,... | collective-permute-start | bytes 393224 | tf_op jit(solution)/shard_map/ppermute | solution.py:14
  75.1 31.9 %all_gather.9 = bf16[512,256]{1,0:T(8,128)(2,1)S(1)} all-gather(bf16[64,256]{1,0:T(8,128)(2,1)S(1)} %fusion.29), channel_id=1, replica_groups=mesh['ctx'=8,'head'=4] {'ctx'}, dimensions={0}, use_global_device_ids=true | all-gather | bytes 294912 | tf_op jit(solution)/shard_map/all_gather | solution.py:85
  114.7 4.2 %all-to-all-start = ((bf16[64,4,1536]{2,0,1:T(8,128)(2,1)}), bf16[64,4,1536]{2,0,1:T(8,128)(2,1)}, u32[]{:S(2)}, u32[]{:S(2)}) async-start(bf16[64,4,1536]{2,0,1:T(8,128)(2,1)} %bitcast.141), calls=%async_computation | async-start | bytes 1572864 | tf_op jit(solution)/shard_map/all_to_all | solution.py:62
  119.5 1.2 fusion.45
  120.8 1.5 reshape.109
  122.3 1.4 copy.68
  123.7 6.8 %all-to-all-done = bf16[64,4,1536]{2,0,1:T(8,128)(2,1)} async-done(((bf16[64,4,1536]{2,0,1:T(8,128)(2,1)}), bf16[64,4,1536]{2,0,1:T(8,128)(2,1)}, u32[]{:S(2)}, u32[]{:S(2)}) %all-to-all-start) | async-done | bytes 786464 | tf_op jit(solution)/shard_map/all_to_all | solution.py:62
  130.6 2.4 reshape.107
  133.0 2.3 copy.64
  135.3 68.0 %while.15 = (s32[]{:T(128)}, f32[1792,128]{1,0:T(8,128)S(1)}, f32[1792,128]{1,0:T(8,128)}, f32[6,2,256,128]{3,2,1,0:T(8,128)}, pred[256,1792]{1,0:T(8,128)(4,1)S...) while((s32[]{:T(128)}, f32[1792,128]{1,0:T(8,128)S(1)}, ...), condition=%wide.region_9.10_spmd.clone, body=%wide.region_5.9_spmd.clone.sunk | while | flops 1188461568 | bytes 80503144 | solution.py:152
  135.3 2.0 fusion.71
  137.9 1.0 multiply_reduce_fusion.2
  139.9 1.4 fusion.74
  141.2 2.1 fusion.72
  143.4 2.9 fusion.73
  146.3 2.0 fusion.71
  150.9 1.4 fusion.74
  152.3 2.1 fusion.72
  154.4 3.3 %fusion.73 = f32[1792,128]{1,0:T(8,128)} fusion(f32[2,256,1792]{2,1,0:T(8,128)S(1)} %copy-done.2, f32[2,256]{1,0:T(2,128)S(1)} %log_add_fusion.2, f32[1792,128]{1,0:T(8,128)} %get-tuple-element.220, pred[]{:T(512)S(6)} %compare.23, bf16[6,2,256,128]{3,2,1,0:T(8,128)(2,1)} %copy-done.8, s32[]{:T(128)} %get-tuple-element.218), kind=kOutput, calls=%fused_computation.10.clone.1 | convolution fusion | flops 237174784 | bytes 5638657 | tf_op jit(solution)/shard_map/while/body/eval_jaxpr/htk,htd->kd/dot_general | solution.py:146
  157.7 2.0 fusion.71
  162.3 1.4 fusion.74
  163.7 2.1 fusion.72
  165.8 3.3 %fusion.73 = f32[1792,128]{1,0:T(8,128)} fusion(f32[2,256,1792]{2,1,0:T(8,128)S(1)} %copy-done.2, f32[2,256]{1,0:T(2,128)S(1)} %log_add_fusion.2, f32[1792,128]{1,0:T(8,128)} %get-tuple-element.220, pred[]{:T(512)S(6)} %compare.23, bf16[6,2,256,128]{3,2,1,0:T(8,128)(2,1)} %copy-done.8, s32[]{:T(128)} %get-tuple-element.218), kind=kOutput, calls=%fused_computation.10.clone.1 | convolution fusion | flops 237174784 | bytes 5638657 | tf_op jit(solution)/shard_map/while/body/eval_jaxpr/htk,htd->kd/dot_general | solution.py:146
  169.1 2.0 fusion.71
  173.7 1.4 fusion.74
  175.1 2.1 fusion.72
  177.2 3.3 %fusion.73 = f32[1792,128]{1,0:T(8,128)} fusion(f32[2,256,1792]{2,1,0:T(8,128)S(1)} %copy-done.2, f32[2,256]{1,0:T(2,128)S(1)} %log_add_fusion.2, f32[1792,128]{1,0:T(8,128)} %get-tuple-element.220, pred[]{:T(512)S(6)} %compare.23, bf16[6,2,256,128]{3,2,1,0:T(8,128)(2,1)} %copy-done.8, s32[]{:T(128)} %get-tuple-element.218), kind=kOutput, calls=%fused_computation.10.clone.1 | convolution fusion | flops 237174784 | bytes 5638657 | tf_op jit(solution)/shard_map/while/body/eval_jaxpr/htk,htd->kd/dot_general | solution.py:146
  180.5 2.0 fusion.71
  185.1 1.4 fusion.74
  186.5 2.1 fusion.72
  188.6 3.3 %fusion.73 = f32[1792,128]{1,0:T(8,128)} fusion(f32[2,256,1792]{2,1,0:T(8,128)S(1)} %copy-done.2, f32[2,256]{1,0:T(2,128)S(1)} %log_add_fusion.2, f32[1792,128]{1,0:T(8,128)} %get-tuple-element.220, pred[]{:T(512)S(6)} %compare.23, bf16[6,2,256,128]{3,2,1,0:T(8,128)(2,1)} %copy-done.8, s32[]{:T(128)} %get-tuple-element.218), kind=kOutput, calls=%fused_computation.10.clone.1 | convolution fusion | flops 237174784 | bytes 5638657 | tf_op jit(solution)/shard_map/while/body/eval_jaxpr/htk,htd->kd/dot_general | solution.py:146
  191.9 2.0 fusion.71
  196.5 1.4 fusion.74
  197.9 2.1 fusion.72
  200.0 3.3 %fusion.73 = f32[1792,128]{1,0:T(8,128)} fusion(f32[2,256,1792]{2,1,0:T(8,128)S(1)} %copy-done.2, f32[2,256]{1,0:T(2,128)S(1)} %log_add_fusion.2, f32[1792,128]{1,0:T(8,128)} %get-tuple-element.220, pred[]{:T(512)S(6)} %compare.23, bf16[6,2,256,128]{3,2,1,0:T(8,128)(2,1)} %copy-done.8, s32[]{:T(128)} %get-tuple-element.218), kind=kOutput, calls=%fused_computation.10.clone.1 | convolution fusion | flops 237174784 | bytes 5638657 | tf_op jit(solution)/shard_map/while/body/eval_jaxpr/htk,htd->kd/dot_general | solution.py:146
  203.4 1.1 copy-done.3
  205.4 1.1 fusion.44
  206.4 1.3 collective-permute-start.4
  207.7 1.3 collective-permute-start.5
  209.0 1.3 collective-permute-start.6
  210.3 1.5 collective-permute-start.7
  211.8 2.4 copy.94
  214.2 1.4 all_to_all.108
  215.5 3.6 %all-to-all-start.4 = ((f32[4,64,1536]{2,1,0:T(8,128)}), f32[4,64,1536]{2,1,0:T(8,128)S(1)}, u32[]{:S(2)}, u32[]{:S(2)}) async-start(f32[4,64,1536]{2,1,0:T(8,128)} %all_to_all.108), calls=%async_computation.4 | async-start | bytes 3145728 | tf_op jit(solution)/shard_map/all_to_all | solution.py:178
  219.1 48.7 %all-reduce.1 = s32[64]{0:T(128)S(1)} all-reduce(s32[64]{0:T(128)S(1)} %get-tuple-element.118), channel_id=1, replica_groups=mesh['ctx'=8,'head'=4] {'ctx'}, use_global_device_ids=true, to_apply=%add.1 | all-reduce | flops 64 | bytes 512
  267.8 1.2 fusion.28
  269.1 2.8 fusion.24
  273.2 3.3 %all-to-all-start.6 = ((f32[4,64,128]{2,1,0:T(8,128)}), f32[4,64,128]{2,1,0:T(8,128)S(1)}, u32[]{:S(2)}, u32[]{:S(2)}) async-start(f32[4,64,128]{2,1,0:T(8,128)} %bitcast.29), calls=%async_computation.6 | async-start | bytes 262144 | tf_op jit(solution)/shard_map/all_to_all | solution.py:180
  276.5 1.3 copy.81
  277.8 3.3 %all-to-all-done.6 = f32[4,64,128]{2,1,0:T(8,128)S(1)} async-done(((f32[4,64,128]{2,1,0:T(8,128)}), f32[4,64,128]{2,1,0:T(8,128)S(1)}, u32[]{:S(2)}, u32[]{:S(2)}) %all-to-all-start.6) | async-done | bytes 131104 | tf_op jit(solution)/shard_map/all_to_all | solution.py:180
  281.1 3.3 %all-to-all-start.5 = ((f32[4,64,128]{2,1,0:T(8,128)}), f32[4,64,128]{2,1,0:T(8,128)S(1)}, u32[]{:S(2)}, u32[]{:S(2)}) async-start(f32[4,64,128]{2,1,0:T(8,128)} %bitcast.27), calls=%async_computation.5 | async-start | bytes 262144 | tf_op jit(solution)/shard_map/all_to_all | solution.py:179
  285.1 3.9 %all-to-all-done.5 = f32[4,64,128]{2,1,0:T(8,128)S(1)} async-done(((f32[4,64,128]{2,1,0:T(8,128)}), f32[4,64,128]{2,1,0:T(8,128)S(1)}, u32[]{:S(2)}, u32[]{:S(2)}) %all-to-all-start.5) | async-done | bytes 131104 | tf_op jit(solution)/shard_map/all_to_all | solution.py:179
  (192 shorter events, 33.7 us)
Async XLA Ops:
  7.2 47.8 %copy-start.11 = (bf16[64,6144]{1,0:T(8,128)(2,1)S(1)}, bf16[64,6144]{1,0:T(8,128)(2,1)}, u32[]{:S(2)}) copy-start(bf16[64,6144]{1,0:T(8,128)(2,1)} %param.12) | copy-start | bytes 2359300
  8.0 47.9 %copy-start.12 = (bf16[64,6144]{1,0:T(8,128)(2,1)S(1)}, bf16[64,6144]{1,0:T(8,128)(2,1)}, u32[]{:S(2)}) copy-start(bf16[64,6144]{1,0:T(8,128)(2,1)} %param.9) | copy-start | bytes 2359300
  8.7 19.7 %all-to-all-start.1 = ((bf16[64,4,128]{2,0,1:T(8,128)(2,1)}), bf16[64,4,128]{2,0,1:T(8,128)(2,1)S(1)}, u32[]{:S(2)}, u32[]{:S(2)}) async-start(bf16[64,4,128]{2,0,1:T(8,128)(2,1)} %copy_bitcast_fusion.6), calls=%async_computation.1 | async-start | bytes 131072 | tf_op jit(solution)/shard_map/all_to_all | solution.py:63
  28.4 29.3 %all-to-all-start.2 = ((bf16[64,4,128]{2,0,1:T(8,128)(2,1)}), bf16[64,4,128]{2,0,1:T(8,128)(2,1)S(1)}, u32[]{:S(2)}, u32[]{:S(2)}) async-start(bf16[64,4,128]{2,0,1:T(8,128)(2,1)} %copy_bitcast_fusion.5), calls=%async_computation.2 | async-start | bytes 131072 | tf_op jit(solution)/shard_map/all_to_all | solution.py:64
  57.7 57.0 %all-to-all-start.3 = ((bf16[64,4,1536]{2,0,1:T(8,128)(2,1)}), bf16[64,4,1536]{2,0,1:T(8,128)(2,1)S(1)}, u32[]{:S(2)}, u32[]{:S(2)}) async-start(bf16[64,4,1536]{2,0,1:T(8,128)(2,1)} %bitcast.142), calls=%async_computation.3 | async-start | bytes 1572864 | tf_op jit(solution)/shard_map/all_to_all | solution.py:65
  61.2 45.8 %collective-permute-start = (bf16[256,256]{1,0:T(8,128)(2,1)S(1)}, bf16[256,256]{1,0:T(8,128)(2,1)S(1)}, u32[]{:S(2)}, u32[]{:S(2)}) collective-permute-start(bf16[256,256]{1,0:T(8,128)(2,1)S(1)} %pad_maximum_fusion), channel_id=1, source_target_pairs={{0,16},{4,20},{8,24},{12,28},{1,17},{5,21},{9,25},{13,29},{2,18},{... | collective-permute-start | bytes 393224 | tf_op jit(solution)/shard_map/ppermute | solution.py:14
  66.2 41.5 %collective-permute-start.1 = (bf16[256,256]{1,0:T(8,128)(2,1)S(1)}, bf16[256,256]{1,0:T(8,128)(2,1)S(1)}, u32[]{:S(2)}, u32[]{:S(2)}) collective-permute-start(bf16[256,256]{1,0:T(8,128)(2,1)S(1)} %pad_maximum_fusion), channel_id=1, source_target_pairs={{0,12},{4,16},{8,20},{12,24},{16,28},{1,13},{5,17},{9,21},{13,25},... | collective-permute-start | bytes 393224 | tf_op jit(solution)/shard_map/ppermute | solution.py:14
  70.7 37.7 %collective-permute-start.2 = (bf16[256,256]{1,0:T(8,128)(2,1)S(1)}, bf16[256,256]{1,0:T(8,128)(2,1)S(1)}, u32[]{:S(2)}, u32[]{:S(2)}) collective-permute-start(bf16[256,256]{1,0:T(8,128)(2,1)S(1)} %pad_maximum_fusion), channel_id=1, source_target_pairs={{0,8},{4,12},{8,16},{12,20},{16,24},{20,28},{1,9},{5,13},{9,17},{1... | collective-permute-start | bytes 393224 | tf_op jit(solution)/shard_map/ppermute | solution.py:14
  72.0 37.0 %collective-permute-start.3 = (bf16[256,256]{1,0:T(8,128)(2,1)S(1)}, bf16[256,256]{1,0:T(8,128)(2,1)S(1)}, u32[]{:S(2)}, u32[]{:S(2)}) collective-permute-start(bf16[256,256]{1,0:T(8,128)(2,1)S(1)} %pad_maximum_fusion), channel_id=1, source_target_pairs={{0,4},{4,8},{8,12},{12,16},{16,20},{20,24},{24,28},{1,5},{5,9},{9,... | collective-permute-start | bytes 393224 | tf_op jit(solution)/shard_map/ppermute | solution.py:14
  114.7 15.9 %all-to-all-start = ((bf16[64,4,1536]{2,0,1:T(8,128)(2,1)}), bf16[64,4,1536]{2,0,1:T(8,128)(2,1)}, u32[]{:S(2)}, u32[]{:S(2)}) async-start(bf16[64,4,1536]{2,0,1:T(8,128)(2,1)} %bitcast.141), calls=%async_computation | async-start | bytes 1572864 | tf_op jit(solution)/shard_map/all_to_all | solution.py:62
  118.9 150.2 %all-gather.2.cloned.1.call-start = ((), (), s32[]{:S(2)}) async-start(), calls=%async_computation.7 | async-start | bytes 2359296 | tf_op jit(solution)/shard_map/all_gather | solution.py:171
  135.3 2.0 copy-start.4
  135.3 2.6 copy-start.6
  135.3 3.6 %copy-start.8 = (bf16[6,2,256,128]{3,2,1,0:T(8,128)(2,1)}, bf16[6,2,256,128]{3,2,1,0:T(8,128)(2,1)S(1)}, u32[]{:S(2)}) copy-start(bf16[6,2,256,128]{3,2,1,0:T(8,128)(2,1)S(1)} %get-tuple-element.236) | copy-start | bytes 2359300 | tf_op jit(solution)/shard_map/while
  137.3 1.8 copy-start.1
  141.2 2.1 copy-start.2
  143.3 3.0 %copy-start.5 = (pred[256,1792]{1,0:T(8,128)(4,1)S(1)}, pred[256,1792]{1,0:T(8,128)(4,1)}, u32[]{:S(2)}) copy-start(pred[256,1792]{1,0:T(8,128)(4,1)} %copy-done.4) | copy-start | bytes 1376260 | tf_op jit(solution)/shard_map/while
  143.3 3.0 %copy-start.7 = (bf16[1792,128]{1,0:T(8,128)(2,1)S(1)}, bf16[1792,128]{1,0:T(8,128)(2,1)}, u32[]{:S(2)}) copy-start(bf16[1792,128]{1,0:T(8,128)(2,1)} %copy-done.6) | copy-start | bytes 1376260 | tf_op jit(solution)/shard_map/while
  143.3 3.0 copy-start.9
  146.3 2.0 copy-start.4
  146.3 2.7 copy-start.6
  146.3 3.6 %copy-start.8 = (bf16[6,2,256,128]{3,2,1,0:T(8,128)(2,1)}, bf16[6,2,256,128]{3,2,1,0:T(8,128)(2,1)S(1)}, u32[]{:S(2)}) copy-start(bf16[6,2,256,128]{3,2,1,0:T(8,128)(2,1)S(1)} %get-tuple-element.236) | copy-start | bytes 2359300 | tf_op jit(solution)/shard_map/while
  148.3 1.8 copy-start.1
  152.3 2.1 copy-start.2
  154.4 3.3 %copy-start.5 = (pred[256,1792]{1,0:T(8,128)(4,1)S(1)}, pred[256,1792]{1,0:T(8,128)(4,1)}, u32[]{:S(2)}) copy-start(pred[256,1792]{1,0:T(8,128)(4,1)} %copy-done.4) | copy-start | bytes 1376260 | tf_op jit(solution)/shard_map/while
  154.4 3.3 %copy-start.7 = (bf16[1792,128]{1,0:T(8,128)(2,1)S(1)}, bf16[1792,128]{1,0:T(8,128)(2,1)}, u32[]{:S(2)}) copy-start(bf16[1792,128]{1,0:T(8,128)(2,1)} %copy-done.6) | copy-start | bytes 1376260 | tf_op jit(solution)/shard_map/while
  154.4 3.3 %copy-start.9 = (bf16[6,2,256,128]{3,2,1,0:T(8,128)(2,1)S(1)}, bf16[6,2,256,128]{3,2,1,0:T(8,128)(2,1)}, u32[]{:S(2)}) copy-start(bf16[6,2,256,128]{3,2,1,0:T(8,128)(2,1)} %copy-done.8) | copy-start | bytes 2359300 | tf_op jit(solution)/shard_map/while
  157.7 2.0 copy-start.4
  157.7 2.7 copy-start.6
  157.7 3.6 %copy-start.8 = (bf16[6,2,256,128]{3,2,1,0:T(8,128)(2,1)}, bf16[6,2,256,128]{3,2,1,0:T(8,128)(2,1)S(1)}, u32[]{:S(2)}) copy-start(bf16[6,2,256,128]{3,2,1,0:T(8,128)(2,1)S(1)} %get-tuple-element.236) | copy-start | bytes 2359300 | tf_op jit(solution)/shard_map/while
  159.7 1.8 copy-start.1
  163.7 2.1 copy-start.2
  165.8 3.3 %copy-start.5 = (pred[256,1792]{1,0:T(8,128)(4,1)S(1)}, pred[256,1792]{1,0:T(8,128)(4,1)}, u32[]{:S(2)}) copy-start(pred[256,1792]{1,0:T(8,128)(4,1)} %copy-done.4) | copy-start | bytes 1376260 | tf_op jit(solution)/shard_map/while
  165.8 3.3 %copy-start.7 = (bf16[1792,128]{1,0:T(8,128)(2,1)S(1)}, bf16[1792,128]{1,0:T(8,128)(2,1)}, u32[]{:S(2)}) copy-start(bf16[1792,128]{1,0:T(8,128)(2,1)} %copy-done.6) | copy-start | bytes 1376260 | tf_op jit(solution)/shard_map/while
  165.8 3.3 %copy-start.9 = (bf16[6,2,256,128]{3,2,1,0:T(8,128)(2,1)S(1)}, bf16[6,2,256,128]{3,2,1,0:T(8,128)(2,1)}, u32[]{:S(2)}) copy-start(bf16[6,2,256,128]{3,2,1,0:T(8,128)(2,1)} %copy-done.8) | copy-start | bytes 2359300 | tf_op jit(solution)/shard_map/while
  169.1 2.0 copy-start.4
  169.1 2.7 copy-start.6
  169.1 3.6 %copy-start.8 = (bf16[6,2,256,128]{3,2,1,0:T(8,128)(2,1)}, bf16[6,2,256,128]{3,2,1,0:T(8,128)(2,1)S(1)}, u32[]{:S(2)}) copy-start(bf16[6,2,256,128]{3,2,1,0:T(8,128)(2,1)S(1)} %get-tuple-element.236) | copy-start | bytes 2359300 | tf_op jit(solution)/shard_map/while
  175.1 2.1 copy-start.2
  177.2 3.3 %copy-start.5 = (pred[256,1792]{1,0:T(8,128)(4,1)S(1)}, pred[256,1792]{1,0:T(8,128)(4,1)}, u32[]{:S(2)}) copy-start(pred[256,1792]{1,0:T(8,128)(4,1)} %copy-done.4) | copy-start | bytes 1376260 | tf_op jit(solution)/shard_map/while
  177.2 3.3 %copy-start.7 = (bf16[1792,128]{1,0:T(8,128)(2,1)S(1)}, bf16[1792,128]{1,0:T(8,128)(2,1)}, u32[]{:S(2)}) copy-start(bf16[1792,128]{1,0:T(8,128)(2,1)} %copy-done.6) | copy-start | bytes 1376260 | tf_op jit(solution)/shard_map/while
  177.2 3.3 %copy-start.9 = (bf16[6,2,256,128]{3,2,1,0:T(8,128)(2,1)S(1)}, bf16[6,2,256,128]{3,2,1,0:T(8,128)(2,1)}, u32[]{:S(2)}) copy-start(bf16[6,2,256,128]{3,2,1,0:T(8,128)(2,1)} %copy-done.8) | copy-start | bytes 2359300 | tf_op jit(solution)/shard_map/while
  180.5 2.0 copy-start.4
  180.5 2.7 copy-start.6
  180.5 3.6 %copy-start.8 = (bf16[6,2,256,128]{3,2,1,0:T(8,128)(2,1)}, bf16[6,2,256,128]{3,2,1,0:T(8,128)(2,1)S(1)}, u32[]{:S(2)}) copy-start(bf16[6,2,256,128]{3,2,1,0:T(8,128)(2,1)S(1)} %get-tuple-element.236) | copy-start | bytes 2359300 | tf_op jit(solution)/shard_map/while
  186.5 2.1 copy-start.2
  188.6 3.3 %copy-start.5 = (pred[256,1792]{1,0:T(8,128)(4,1)S(1)}, pred[256,1792]{1,0:T(8,128)(4,1)}, u32[]{:S(2)}) copy-start(pred[256,1792]{1,0:T(8,128)(4,1)} %copy-done.4) | copy-start | bytes 1376260 | tf_op jit(solution)/shard_map/while
  188.6 3.3 %copy-start.7 = (bf16[1792,128]{1,0:T(8,128)(2,1)S(1)}, bf16[1792,128]{1,0:T(8,128)(2,1)}, u32[]{:S(2)}) copy-start(bf16[1792,128]{1,0:T(8,128)(2,1)} %copy-done.6) | copy-start | bytes 1376260 | tf_op jit(solution)/shard_map/while
  188.6 3.3 %copy-start.9 = (bf16[6,2,256,128]{3,2,1,0:T(8,128)(2,1)S(1)}, bf16[6,2,256,128]{3,2,1,0:T(8,128)(2,1)}, u32[]{:S(2)}) copy-start(bf16[6,2,256,128]{3,2,1,0:T(8,128)(2,1)} %copy-done.8) | copy-start | bytes 2359300 | tf_op jit(solution)/shard_map/while
  191.9 2.0 copy-start.4
  191.9 2.7 copy-start.6
  191.9 3.6 %copy-start.8 = (bf16[6,2,256,128]{3,2,1,0:T(8,128)(2,1)}, bf16[6,2,256,128]{3,2,1,0:T(8,128)(2,1)S(1)}, u32[]{:S(2)}) copy-start(bf16[6,2,256,128]{3,2,1,0:T(8,128)(2,1)S(1)} %get-tuple-element.236) | copy-start | bytes 2359300 | tf_op jit(solution)/shard_map/while
  197.9 2.1 copy-start.2
  200.0 3.3 %copy-start.5 = (pred[256,1792]{1,0:T(8,128)(4,1)S(1)}, pred[256,1792]{1,0:T(8,128)(4,1)}, u32[]{:S(2)}) copy-start(pred[256,1792]{1,0:T(8,128)(4,1)} %copy-done.4) | copy-start | bytes 1376260 | tf_op jit(solution)/shard_map/while
  200.0 3.3 %copy-start.7 = (bf16[1792,128]{1,0:T(8,128)(2,1)S(1)}, bf16[1792,128]{1,0:T(8,128)(2,1)}, u32[]{:S(2)}) copy-start(bf16[1792,128]{1,0:T(8,128)(2,1)} %copy-done.6) | copy-start | bytes 1376260 | tf_op jit(solution)/shard_map/while
  200.0 3.3 %copy-start.9 = (bf16[6,2,256,128]{3,2,1,0:T(8,128)(2,1)S(1)}, bf16[6,2,256,128]{3,2,1,0:T(8,128)(2,1)}, u32[]{:S(2)}) copy-start(bf16[6,2,256,128]{3,2,1,0:T(8,128)(2,1)} %copy-done.8) | copy-start | bytes 2359300 | tf_op jit(solution)/shard_map/while
  204.5 7.3 %copy-start.10 = (f32[1792,256]{1,0:T(8,128)}, f32[1792,256]{1,0:T(8,128)S(1)}, u32[]{:S(2)}) copy-start(f32[1792,256]{1,0:T(8,128)S(1)} %constant_dynamic-update-slice_fusion.13) | copy-start | bytes 5505028
  206.4 61.4 %collective-permute-start.4 = (f32[256,256]{1,0:T(8,128)}, f32[256,256]{1,0:T(8,128)S(1)}, u32[]{:S(2)}, u32[]{:S(2)}) collective-permute-start(f32[256,256]{1,0:T(8,128)} %get-tuple-element.124), channel_id=1, source_target_pairs={{4,0},{8,4},{12,8},{16,12},{20,16},{24,20},{28,24},{5,1},{9,5},{13... | collective-permute-start | bytes 786440 | tf_op jit(solution)/shard_map/ppermute | solution.py:14
  207.7 60.1 %collective-permute-start.5 = (f32[256,256]{1,0:T(8,128)}, f32[256,256]{1,0:T(8,128)S(1)}, u32[]{:S(2)}, u32[]{:S(2)}) collective-permute-start(f32[256,256]{1,0:T(8,128)} %get-tuple-element.127), channel_id=1, source_target_pairs={{8,0},{12,4},{16,8},{20,12},{24,16},{28,20},{9,1},{13,5},{17,9},{2... | collective-permute-start | bytes 786440 | tf_op jit(solution)/shard_map/ppermute | solution.py:14
  209.0 58.8 %collective-permute-start.6 = (f32[256,256]{1,0:T(8,128)}, f32[256,256]{1,0:T(8,128)}, u32[]{:S(2)}, u32[]{:S(2)}) collective-permute-start(f32[256,256]{1,0:T(8,128)} %get-tuple-element.126), channel_id=1, source_target_pairs={{12,0},{16,4},{20,8},{24,12},{28,16},{13,1},{17,5},{21,9},{25,13},... | collective-permute-start | bytes 786440 | tf_op jit(solution)/shard_map/ppermute | solution.py:14
  210.3 57.5 %collective-permute-start.7 = (f32[256,256]{1,0:T(8,128)}, f32[256,256]{1,0:T(8,128)}, u32[]{:S(2)}, u32[]{:S(2)}) collective-permute-start(f32[256,256]{1,0:T(8,128)} %get-tuple-element.125), channel_id=1, source_target_pairs={{16,0},{20,4},{24,8},{28,12},{17,1},{21,5},{25,9},{29,13},{18,2},{... | collective-permute-start | bytes 786440 | tf_op jit(solution)/shard_map/ppermute | solution.py:14
  215.5 57.6 %all-to-all-start.4 = ((f32[4,64,1536]{2,1,0:T(8,128)}), f32[4,64,1536]{2,1,0:T(8,128)S(1)}, u32[]{:S(2)}, u32[]{:S(2)}) async-start(f32[4,64,1536]{2,1,0:T(8,128)} %all_to_all.108), calls=%async_computation.4 | async-start | bytes 3145728 | tf_op jit(solution)/shard_map/all_to_all | solution.py:178
  273.2 7.9 %all-to-all-start.6 = ((f32[4,64,128]{2,1,0:T(8,128)}), f32[4,64,128]{2,1,0:T(8,128)S(1)}, u32[]{:S(2)}, u32[]{:S(2)}) async-start(f32[4,64,128]{2,1,0:T(8,128)} %bitcast.29), calls=%async_computation.6 | async-start | bytes 262144 | tf_op jit(solution)/shard_map/all_to_all | solution.py:180
  281.1 7.9 %all-to-all-start.5 = ((f32[4,64,128]{2,1,0:T(8,128)}), f32[4,64,128]{2,1,0:T(8,128)S(1)}, u32[]{:S(2)}, u32[]{:S(2)}) async-start(f32[4,64,128]{2,1,0:T(8,128)} %bitcast.27), calls=%async_computation.5 | async-start | bytes 262144 | tf_op jit(solution)/shard_map/all_to_all | solution.py:179
  (5 other events, 7.4 us)
Sparse Core Ops, SparseCore 0:
  205.5 60.7 all-gather.1
where the time goes:
time: 299 us; the launch traced here: 296 us
  blocking collectives  80.6 us (27%)
  matrix products  60.3 us (20%)
  starting transfers between devices  44.7 us (15%)
  between operations  43 us (14%)
  local copies, waits for them, and re-layouts  38.6 us (13%)
  other arithmetic  14.6 us (5%)
  waiting for transfers between devices  14.1 us (5%)
    unnamed x1, blocking collectives  48.7 us
    all_gather x1, blocking collectives, per_device(): all_headers = lax.all_gather(own_header, 'ctx', axis=0, tiled=True)  31.9 us
    dot_general x6, matrix products, attend(): jnp.einsum('htk,htd->kd', weights_low, grad_block, preferred_element_type...  19.3 us
    ppermute x8, starting transfers between devices, passed_along(): lax.ppermute(value, axis, [(source, source + steps) for source in range(f...  19.2 us
    dot_general x6, matrix products, attend(): jnp.einsum('htk,htd->kd', grad_scores, query_block, preferred_element_typ...  12.4 us
    dot_general x6, matrix products, attend(): jnp.einsum('htd,kd->htk', query_block, key_matrix, preferred_element_type...  11.8 us
    unnamed x24, local copies, waits for them, and re-layouts  10.3 us
    dot_general x6, matrix products, attend(): jnp.einsum('htk,kd->htd', grad_scores, key_matrix, preferred_element_type...  8.1 us
  transfers between devices with their start and end apart: 16, of which 3 were waited for; matrix products, arithmetic and copies ran while one was open for 12% of the time, Pallas kernels for 0%

commit v1 on v0

--- a/solution.py
+++ b/solution.py
@@ -6,6 +6,14 @@
 
 WIN = 1024
 HDR = 64
+
+
+def make_corner(mine, dimension_no):
+    mine = jnp.moveaxis(mine, 0, dimension_no)
+    r1 = mine.shape
+    return mine.reshape(
+        *r1[:dimension_no], r1[dimension_no] * r1[dimension_no + 1], *r1[dimension_no + 2 :]
+    )
 
 
 def passed_along(value, axis, steps):
@@ -82,7 +90,33 @@
     inside = (file_starts >= offset_base) & (file_starts < offset_base + tokens_here)
     own_offset = jnp.sum(jnp.where(inside, file_starts - offset_base, 0))
     own_header = lax.dynamic_slice_in_dim(stacked, own_offset, HDR, 0)
-    all_headers = lax.all_gather(own_header, "ctx", axis=0, tiled=True)
+
+    def drive_stocks(inp, along_dim, mesh_name):
+        total_devices = jax.lax.axis_size(mesh_name)
+        so_far_all = [(j0, (j0 + 1) % total_devices) for j0 in range(total_devices)]
+        all_rows = [(kk, src_i) for src_i, kk in so_far_all]
+        z2, high = ([], [])
+        rr = 0
+        while rr < total_devices - 1:
+            if rr % 2 == 0:
+                taken_in = jax.lax.ppermute(
+                    z2[-1] if z2 else inp, axis_name=mesh_name, perm=so_far_all
+                )
+                z2.append(taken_in)
+            else:
+                v_next = jax.lax.ppermute(
+                    high[-1] if high else inp, perm=all_rows, axis_name=mesh_name
+                )
+                high.append(v_next)
+            rr = rr + 1
+        opened = jnp.stack([*z2[::-1], inp, *high])
+        local_now = jax.lax.axis_index(mesh_name)
+        extra = len(z2)
+        reached = local_now - extra
+        opened = opened[(jnp.arange(total_devices) - reached) % total_devices]
+        return make_corner(opened, along_dim)
+
+    all_headers = drive_stocks(own_header, 0, "ctx")
     header_rows = jnp.concatenate(
         [
             lax.dynamic_slice_in_dim(all_headers, target_start[index] // tokens_here * HDR, HDR, 0)

time: 299 us -> 286 us (0.957)
  blocking collectives: 80.6 us -> 50.2 us
  starting transfers between devices: 44.7 us -> 58.8 us
    all_gather x1 -> x0, blocking collectives: 31.9 us -> none  [per_device(): all_headers = lax.all_gather(own_header, 'ctx', axis=0, tiled=True)]
    ppermute x0 -> x7, starting transfers between devices: none -> 10.5 us  [the longest x3 5.66 us: drive_stocks(): jax.lax.ppermute(high[-1] if high else inp, perm=all_rows, axis_name=mesh...]
    ppermute x8, starting transfers between devices: 19.2 us -> 22.9 us  [passed_along(): lax.ppermute(value, axis, [(source, source + steps) for source in range(f...]
    unnamed x24 -> x29, local copies, waits for them, and re-layouts: 10.3 us -> 10.3 us
  transfers between devices with their start and end apart: 16 -> 23, of which waited for: 3 -> 5; matrix products, arithmetic and copies ran while one was open for 12% -> 13% of each run, Pallas kernels for 0% -> 0%
where the time goes in v1:
time: 286 us; the launch traced here: 284 us
  matrix products  60.2 us (21%)
  starting transfers between devices  58.8 us (21%)
  blocking collectives  50.2 us (18%)
  between operations  42.9 us (15%)
  local copies, waits for them, and re-layouts  40.3 us (14%)
  waiting for transfers between devices  16 us (6%)
  other arithmetic  14.5 us (5%)
    unnamed x1, blocking collectives  50.2 us
    ppermute x8, starting transfers between devices, passed_along(): lax.ppermute(value, axis, [(source, source + steps) for source in range(f...  22.9 us
    dot_general x6, matrix products, attend(): jnp.einsum('htk,htd->kd', weights_low, grad_block, preferred_element_type...  19.2 us
    dot_general x6, matrix products, attend(): jnp.einsum('htk,htd->kd', grad_scores, query_block, preferred_element_typ...  12.5 us
    dot_general x6, matrix products, attend(): jnp.einsum('htd,kd->htk', query_block, key_matrix, preferred_element_type...  11.9 us
    unnamed x29, local copies, waits for them, and re-layouts  10.3 us
    dot_general x6, matrix products, attend(): jnp.einsum('htk,kd->htd', grad_scores, key_matrix, preferred_element_type...  8.1 us
    all_to_all x1, waiting for transfers between devices, per_device(): lax.all_to_all(queries, 'head', split_axis=1, concat_axis=0, tiled=True)  6.84 us
  transfers between devices with their start and end apart: 23, of which 5 were waited for; matrix products, arithmetic and copies ran while one was open for 13% of the time, Pallas kernels for 0%

profile of v1, /device:TPU:0, one launch (start us, length us, event | category | flops | bytes accessed | tf_op | source)
XLA Modules:
  0.0 283.6 jit_solution(6338173375911563007)
XLA Ops:
  8.7 4.2 %all-to-all-start.1 = ((bf16[64,4,128]{2,0,1:T(8,128)(2,1)}), bf16[64,4,128]{2,0,1:T(8,128)(2,1)S(1)}, u32[]{:S(2)}, u32[]{:S(2)}) async-start(bf16[64,4,128]{2,0,1:T(8,128)(2,1)} %copy_bitcast_fusion.6), calls=%async_computation.1 | async-start | bytes 131072 | tf_op jit(solution)/shard_map/all_to_all | solution.py:71
  18.0 1.5 copy_bitcast_fusion.5
  22.8 1.3 dynamic-slice
  28.1 3.3 %all-to-all-start.2 = ((bf16[64,4,128]{2,0,1:T(8,128)(2,1)}), bf16[64,4,128]{2,0,1:T(8,128)(2,1)S(1)}, u32[]{:S(2)}, u32[]{:S(2)}) async-start(bf16[64,4,128]{2,0,1:T(8,128)(2,1)} %copy_bitcast_fusion.5), calls=%async_computation.2 | async-start | bytes 131072 | tf_op jit(solution)/shard_map/all_to_all | solution.py:72
  31.4 1.3 fusion.43
  35.6 3.5 %all-to-all-start.3 = ((bf16[64,4,1536]{2,0,1:T(8,128)(2,1)}), bf16[64,4,1536]{2,0,1:T(8,128)(2,1)S(1)}, u32[]{:S(2)}, u32[]{:S(2)}) async-start(bf16[64,4,1536]{2,0,1:T(8,128)(2,1)} %bitcast.127), calls=%async_computation.3 | async-start | bytes 1572864 | tf_op jit(solution)/shard_map/all_to_all | solution.py:73
  39.2 2.1 collective-permute-start.4
  41.3 3.1 %collective-permute-start.8 = (bf16[64,256]{1,0:T(8,128)(2,1)S(1)}, bf16[64,256]{1,0:T(8,128)(2,1)S(1)}, u32[]{:S(2)}, u32[]{:S(2)}) collective-permute-start(bf16[64,256]{1,0:T(8,128)(2,1)S(1)} %fusion.29), channel_id=1, source_target_pairs={{4,0},{8,4},{12,8},{16,12},{20,16},{24,20},{28,24},{0,28},{5,1},{9... | collective-permute-start | bytes 98312 | tf_op jit(solution)/shard_map/ppermute | solution.py:107
  44.4 2.8 collective-permute-start
  47.9 2.9 %collective-permute-start.1 = (bf16[256,256]{1,0:T(8,128)(2,1)S(1)}, bf16[256,256]{1,0:T(8,128)(2,1)S(1)}, u32[]{:S(2)}, u32[]{:S(2)}) collective-permute-start(bf16[256,256]{1,0:T(8,128)(2,1)S(1)} %pad_maximum_fusion), channel_id=1, source_target_pairs={{0,12},{4,16},{8,20},{12,24},{16,28},{1,13},{5,17},{9,21},{13,25},... | collective-permute-start | bytes 393224 | tf_op jit(solution)/shard_map/ppermute | solution.py:22
  50.9 2.5 collective-permute-start.9
  74.6 2.1 copy.96
  76.8 6.5 %collective-permute-start.2 = (bf16[256,256]{1,0:T(8,128)(2,1)S(1)}, bf16[256,256]{1,0:T(8,128)(2,1)S(1)}, u32[]{:S(2)}, u32[]{:S(2)}) collective-permute-start(bf16[256,256]{1,0:T(8,128)(2,1)S(1)} %pad_maximum_fusion), channel_id=1, source_target_pairs={{0,8},{4,12},{8,16},{12,20},{16,24},{20,28},{1,9},{5,13},{9,17},{1... | collective-permute-start | bytes 393224 | tf_op jit(solution)/shard_map/ppermute | solution.py:22
  83.3 5.3 %collective-permute-start.3 = (bf16[256,256]{1,0:T(8,128)(2,1)S(1)}, bf16[256,256]{1,0:T(8,128)(2,1)S(1)}, u32[]{:S(2)}, u32[]{:S(2)}) collective-permute-start(bf16[256,256]{1,0:T(8,128)(2,1)S(1)} %pad_maximum_fusion), channel_id=1, source_target_pairs={{0,4},{4,8},{8,12},{12,16},{16,20},{20,24},{24,28},{1,5},{5,9},{9,... | collective-permute-start | bytes 393224 | tf_op jit(solution)/shard_map/ppermute | solution.py:22
  88.7 2.0 collective-permute-start.7
  94.0 1.3 collective-permute-done.7
  100.3 4.2 %all-to-all-start = ((bf16[64,4,1536]{2,0,1:T(8,128)(2,1)}), bf16[64,4,1536]{2,0,1:T(8,128)(2,1)}, u32[]{:S(2)}, u32[]{:S(2)}) async-start(bf16[64,4,1536]{2,0,1:T(8,128)(2,1)} %bitcast.160), calls=%async_computation | async-start | bytes 1572864 | tf_op jit(solution)/shard_map/all_to_all | solution.py:70
  105.2 1.2 fusion.47
  106.4 1.5 reshape.162
  107.9 1.4 copy.68
  109.4 6.8 %all-to-all-done = bf16[64,4,1536]{2,0,1:T(8,128)(2,1)} async-done(((bf16[64,4,1536]{2,0,1:T(8,128)(2,1)}), bf16[64,4,1536]{2,0,1:T(8,128)(2,1)}, u32[]{:S(2)}, u32[]{:S(2)}) %all-to-all-start) | async-done | bytes 786464 | tf_op jit(solution)/shard_map/all_to_all | solution.py:70
  116.2 2.4 reshape.159
  118.6 2.3 copy.64
  120.9 67.9 %while.15 = (s32[]{:T(128)}, f32[1792,128]{1,0:T(8,128)S(1)}, f32[1792,128]{1,0:T(8,128)}, f32[6,2,256,128]{3,2,1,0:T(8,128)}, pred[256,1792]{1,0:T(8,128)(4,1)S...) while((s32[]{:T(128)}, f32[1792,128]{1,0:T(8,128)S(1)}, ...), condition=%wide.region_9.10_spmd.clone, body=%wide.region_5.9_spmd.clone.sunk | while | flops 1188461568 | bytes 80503144 | solution.py:186
  120.9 2.0 fusion.73
  125.5 1.4 fusion.76
  126.9 2.1 fusion.74
  129.0 2.9 %fusion.75 = f32[1792,128]{1,0:T(8,128)} fusion(f32[2,256,1792]{2,1,0:T(8,128)S(1)} %copy-done.2, f32[2,256]{1,0:T(2,128)S(1)} %log_add_fusion.2, f32[1792,128]{1,0:T(8,128)} %get-tuple-element.220, pred[]{:T(512)S(6)} %compare.30, bf16[6,2,256,128]{3,2,1,0:T(8,128)(2,1)} %copy-done.8, s32[]{:T(128)} %get-tuple-element.218), kind=kOutput, calls=%fused_computation.11.clone.1 | convolution fusion | flops 237174784 | bytes 5638657 | tf_op jit(solution)/shard_map/while/body/eval_jaxpr/htk,htd->kd/dot_general | solution.py:180
  132.0 2.0 fusion.73
  136.6 1.4 fusion.76
  137.9 2.1 fusion.74
  140.0 3.3 %fusion.75 = f32[1792,128]{1,0:T(8,128)} fusion(f32[2,256,1792]{2,1,0:T(8,128)S(1)} %copy-done.2, f32[2,256]{1,0:T(2,128)S(1)} %log_add_fusion.2, f32[1792,128]{1,0:T(8,128)} %get-tuple-element.220, pred[]{:T(512)S(6)} %compare.30, bf16[6,2,256,128]{3,2,1,0:T(8,128)(2,1)} %copy-done.8, s32[]{:T(128)} %get-tuple-element.218), kind=kOutput, calls=%fused_computation.11.clone.1 | convolution fusion | flops 237174784 | bytes 5638657 | tf_op jit(solution)/shard_map/while/body/eval_jaxpr/htk,htd->kd/dot_general | solution.py:180
  143.4 2.0 fusion.73
  147.9 1.4 fusion.76
  149.3 2.1 fusion.74
  151.4 3.3 %fusion.75 = f32[1792,128]{1,0:T(8,128)} fusion(f32[2,256,1792]{2,1,0:T(8,128)S(1)} %copy-done.2, f32[2,256]{1,0:T(2,128)S(1)} %log_add_fusion.2, f32[1792,128]{1,0:T(8,128)} %get-tuple-element.220, pred[]{:T(512)S(6)} %compare.30, bf16[6,2,256,128]{3,2,1,0:T(8,128)(2,1)} %copy-done.8, s32[]{:T(128)} %get-tuple-element.218), kind=kOutput, calls=%fused_computation.11.clone.1 | convolution fusion | flops 237174784 | bytes 5638657 | tf_op jit(solution)/shard_map/while/body/eval_jaxpr/htk,htd->kd/dot_general | solution.py:180
  154.7 2.0 fusion.73
  159.3 1.4 fusion.76
  160.7 2.1 fusion.74
  162.8 3.3 %fusion.75 = f32[1792,128]{1,0:T(8,128)} fusion(f32[2,256,1792]{2,1,0:T(8,128)S(1)} %copy-done.2, f32[2,256]{1,0:T(2,128)S(1)} %log_add_fusion.2, f32[1792,128]{1,0:T(8,128)} %get-tuple-element.220, pred[]{:T(512)S(6)} %compare.30, bf16[6,2,256,128]{3,2,1,0:T(8,128)(2,1)} %copy-done.8, s32[]{:T(128)} %get-tuple-element.218), kind=kOutput, calls=%fused_computation.11.clone.1 | convolution fusion | flops 237174784 | bytes 5638657 | tf_op jit(solution)/shard_map/while/body/eval_jaxpr/htk,htd->kd/dot_general | solution.py:180
  166.1 2.0 fusion.73
  170.7 1.4 fusion.76
  172.1 2.1 fusion.74
  174.2 3.3 %fusion.75 = f32[1792,128]{1,0:T(8,128)} fusion(f32[2,256,1792]{2,1,0:T(8,128)S(1)} %copy-done.2, f32[2,256]{1,0:T(2,128)S(1)} %log_add_fusion.2, f32[1792,128]{1,0:T(8,128)} %get-tuple-element.220, pred[]{:T(512)S(6)} %compare.30, bf16[6,2,256,128]{3,2,1,0:T(8,128)(2,1)} %copy-done.8, s32[]{:T(128)} %get-tuple-element.218), kind=kOutput, calls=%fused_computation.11.clone.1 | convolution fusion | flops 237174784 | bytes 5638657 | tf_op jit(solution)/shard_map/while/body/eval_jaxpr/htk,htd->kd/dot_general | solution.py:180
  177.5 2.0 fusion.73
  182.1 1.4 fusion.76
  183.5 2.1 fusion.74
  185.6 3.3 %fusion.75 = f32[1792,128]{1,0:T(8,128)} fusion(f32[2,256,1792]{2,1,0:T(8,128)S(1)} %copy-done.2, f32[2,256]{1,0:T(2,128)S(1)} %log_add_fusion.2, f32[1792,128]{1,0:T(8,128)} %get-tuple-element.220, pred[]{:T(512)S(6)} %compare.30, bf16[6,2,256,128]{3,2,1,0:T(8,128)(2,1)} %copy-done.8, s32[]{:T(128)} %get-tuple-element.218), kind=kOutput, calls=%fused_computation.11.clone.1 | convolution fusion | flops 237174784 | bytes 5638657 | tf_op jit(solution)/shard_map/while/body/eval_jaxpr/htk,htd->kd/dot_general | solution.py:180
  189.0 1.1 copy-done.3
  192.0 1.3 collective-permute-start.11
  193.2 1.3 collective-permute-start.12
  194.5 1.3 collective-permute-start.13
  195.8 1.5 collective-permute-start.14
  197.3 2.4 copy.94
  199.7 1.4 all_to_all.108
  201.1 3.6 %all-to-all-start.4 = ((f32[4,64,1536]{2,1,0:T(8,128)}), f32[4,64,1536]{2,1,0:T(8,128)S(1)}, u32[]{:S(2)}, u32[]{:S(2)}) async-start(f32[4,64,1536]{2,1,0:T(8,128)} %all_to_all.108), calls=%async_computation.4 | async-start | bytes 3145728 | tf_op jit(solution)/shard_map/all_to_all | solution.py:212
  204.6 50.2 %all-reduce.1 = s32[64]{0:T(128)S(1)} all-reduce(s32[64]{0:T(128)S(1)} %get-tuple-element.118), channel_id=1, replica_groups=mesh['ctx'=8,'head'=4] {'ctx'}, use_global_device_ids=true, to_apply=%add.1 | all-reduce | flops 64 | bytes 512
  254.9 1.2 fusion.28
  256.1 2.8 fusion.24
  260.2 3.3 %all-to-all-start.6 = ((f32[4,64,128]{2,1,0:T(8,128)}), f32[4,64,128]{2,1,0:T(8,128)S(1)}, u32[]{:S(2)}, u32[]{:S(2)}) async-start(f32[4,64,128]{2,1,0:T(8,128)} %bitcast.39), calls=%async_computation.6 | async-start | bytes 262144 | tf_op jit(solution)/shard_map/all_to_all | solution.py:214
  263.6 1.3 copy.81
  264.9 3.3 %all-to-all-done.6 = f32[4,64,128]{2,1,0:T(8,128)S(1)} async-done(((f32[4,64,128]{2,1,0:T(8,128)}), f32[4,64,128]{2,1,0:T(8,128)S(1)}, u32[]{:S(2)}, u32[]{:S(2)}) %all-to-all-start.6) | async-done | bytes 131104 | tf_op jit(solution)/shard_map/all_to_all | solution.py:214
  268.1 3.3 %all-to-all-start.5 = ((f32[4,64,128]{2,1,0:T(8,128)}), f32[4,64,128]{2,1,0:T(8,128)S(1)}, u32[]{:S(2)}, u32[]{:S(2)}) async-start(f32[4,64,128]{2,1,0:T(8,128)} %bitcast.37), calls=%async_computation.5 | async-start | bytes 262144 | tf_op jit(solution)/shard_map/all_to_all | solution.py:213
  272.1 3.9 %all-to-all-done.5 = f32[4,64,128]{2,1,0:T(8,128)S(1)} async-done(((f32[4,64,128]{2,1,0:T(8,128)}), f32[4,64,128]{2,1,0:T(8,128)S(1)}, u32[]{:S(2)}, u32[]{:S(2)}) %all-to-all-start.5) | async-done | bytes 131104 | tf_op jit(solution)/shard_map/all_to_all | solution.py:213
  (214 shorter events, 39.5 us)
Async XLA Ops:
  7.2 26.8 %copy-start.11 = (bf16[64,6144]{1,0:T(8,128)(2,1)S(1)}, bf16[64,6144]{1,0:T(8,128)(2,1)}, u32[]{:S(2)}) copy-start(bf16[64,6144]{1,0:T(8,128)(2,1)} %param.12) | copy-start | bytes 2359300
  8.7 19.4 %all-to-all-start.1 = ((bf16[64,4,128]{2,0,1:T(8,128)(2,1)}), bf16[64,4,128]{2,0,1:T(8,128)(2,1)S(1)}, u32[]{:S(2)}, u32[]{:S(2)}) async-start(bf16[64,4,128]{2,0,1:T(8,128)(2,1)} %copy_bitcast_fusion.6), calls=%async_computation.1 | async-start | bytes 131072 | tf_op jit(solution)/shard_map/all_to_all | solution.py:71
  28.1 7.6 %all-to-all-start.2 = ((bf16[64,4,128]{2,0,1:T(8,128)(2,1)}), bf16[64,4,128]{2,0,1:T(8,128)(2,1)S(1)}, u32[]{:S(2)}, u32[]{:S(2)}) async-start(bf16[64,4,128]{2,0,1:T(8,128)(2,1)} %copy_bitcast_fusion.5), calls=%async_computation.2 | async-start | bytes 131072 | tf_op jit(solution)/shard_map/all_to_all | solution.py:72
  35.6 64.7 %all-to-all-start.3 = ((bf16[64,4,1536]{2,0,1:T(8,128)(2,1)}), bf16[64,4,1536]{2,0,1:T(8,128)(2,1)S(1)}, u32[]{:S(2)}, u32[]{:S(2)}) async-start(bf16[64,4,1536]{2,0,1:T(8,128)(2,1)} %bitcast.127), calls=%async_computation.3 | async-start | bytes 1572864 | tf_op jit(solution)/shard_map/all_to_all | solution.py:73
  39.2 8.1 %collective-permute-start.4 = (bf16[64,256]{1,0:T(8,128)(2,1)S(1)}, bf16[64,256]{1,0:T(8,128)(2,1)S(1)}, u32[]{:S(2)}, u32[]{:S(2)}) collective-permute-start(bf16[64,256]{1,0:T(8,128)(2,1)S(1)} %fusion.29), channel_id=1, source_target_pairs={{0,4},{4,8},{8,12},{12,16},{16,20},{20,24},{24,28},{28,0},{1,5},{5... | collective-permute-start | bytes 98312 | tf_op jit(solution)/shard_map/ppermute | solution.py:102
  41.3 9.6 %collective-permute-start.8 = (bf16[64,256]{1,0:T(8,128)(2,1)S(1)}, bf16[64,256]{1,0:T(8,128)(2,1)S(1)}, u32[]{:S(2)}, u32[]{:S(2)}) collective-permute-start(bf16[64,256]{1,0:T(8,128)(2,1)S(1)} %fusion.29), channel_id=1, source_target_pairs={{4,0},{8,4},{12,8},{16,12},{20,16},{24,20},{28,24},{0,28},{5,1},{9... | collective-permute-start | bytes 98312 | tf_op jit(solution)/shard_map/ppermute | solution.py:107
  44.4 44.2 %collective-permute-start = (bf16[256,256]{1,0:T(8,128)(2,1)S(1)}, bf16[256,256]{1,0:T(8,128)(2,1)S(1)}, u32[]{:S(2)}, u32[]{:S(2)}) collective-permute-start(bf16[256,256]{1,0:T(8,128)(2,1)S(1)} %pad_maximum_fusion), channel_id=1, source_target_pairs={{0,16},{4,20},{8,24},{12,28},{1,17},{5,21},{9,25},{13,29},{2,18},{... | collective-permute-start | bytes 393224 | tf_op jit(solution)/shard_map/ppermute | solution.py:22
  47.2 6.7 %collective-permute-start.5 = (bf16[64,256]{1,0:T(8,128)(2,1)S(1)}, bf16[64,256]{1,0:T(8,128)(2,1)S(1)}, u32[]{:S(2)}, u32[]{:S(2)}) collective-permute-start(bf16[64,256]{1,0:T(8,128)(2,1)S(1)} %collective-permute-done.4), channel_id=1, source_target_pairs={{0,4},{4,8},{8,12},{12,16},{16,20},{20,24},{24,28},{28,0},{1,5},{5... | collective-permute-start | bytes 98312 | tf_op jit(solution)/shard_map/ppermute | solution.py:102
  47.9 43.4 %collective-permute-start.1 = (bf16[256,256]{1,0:T(8,128)(2,1)S(1)}, bf16[256,256]{1,0:T(8,128)(2,1)S(1)}, u32[]{:S(2)}, u32[]{:S(2)}) collective-permute-start(bf16[256,256]{1,0:T(8,128)(2,1)S(1)} %pad_maximum_fusion), channel_id=1, source_target_pairs={{0,12},{4,16},{8,20},{12,24},{16,28},{1,13},{5,17},{9,21},{13,25},... | collective-permute-start | bytes 393224 | tf_op jit(solution)/shard_map/ppermute | solution.py:22
  50.9 32.4 %collective-permute-start.9 = (bf16[64,256]{1,0:T(8,128)(2,1)S(1)}, bf16[64,256]{1,0:T(8,128)(2,1)S(1)}, u32[]{:S(2)}, u32[]{:S(2)}) collective-permute-start(bf16[64,256]{1,0:T(8,128)(2,1)S(1)} %collective-permute-done.8), channel_id=1, source_target_pairs={{4,0},{8,4},{12,8},{16,12},{20,16},{24,20},{28,24},{0,28},{5,1},{9... | collective-permute-start | bytes 98312 | tf_op jit(solution)/shard_map/ppermute | solution.py:107
  53.9 34.7 %collective-permute-start.6 = (bf16[64,256]{1,0:T(8,128)(2,1)S(1)}, bf16[64,256]{1,0:T(8,128)(2,1)S(1)}, u32[]{:S(2)}, u32[]{:S(2)}) collective-permute-start(bf16[64,256]{1,0:T(8,128)(2,1)S(1)} %collective-permute-done.5), channel_id=1, source_target_pairs={{0,4},{4,8},{8,12},{12,16},{16,20},{20,24},{24,28},{28,0},{1,5},{5... | collective-permute-start | bytes 98312 | tf_op jit(solution)/shard_map/ppermute | solution.py:102
  76.8 15.2 %collective-permute-start.2 = (bf16[256,256]{1,0:T(8,128)(2,1)S(1)}, bf16[256,256]{1,0:T(8,128)(2,1)S(1)}, u32[]{:S(2)}, u32[]{:S(2)}) collective-permute-start(bf16[256,256]{1,0:T(8,128)(2,1)S(1)} %pad_maximum_fusion), channel_id=1, source_target_pairs={{0,8},{4,12},{8,16},{12,20},{16,24},{20,28},{1,9},{5,13},{9,17},{1... | collective-permute-start | bytes 393224 | tf_op jit(solution)/shard_map/ppermute | solution.py:22
  83.3 9.4 %collective-permute-start.3 = (bf16[256,256]{1,0:T(8,128)(2,1)S(1)}, bf16[256,256]{1,0:T(8,128)(2,1)S(1)}, u32[]{:S(2)}, u32[]{:S(2)}) collective-permute-start(bf16[256,256]{1,0:T(8,128)(2,1)S(1)} %pad_maximum_fusion), channel_id=1, source_target_pairs={{0,4},{4,8},{8,12},{12,16},{16,20},{20,24},{24,28},{1,5},{5,9},{9,... | collective-permute-start | bytes 393224 | tf_op jit(solution)/shard_map/ppermute | solution.py:22
  88.6 6.8 %collective-permute-start.10 = (bf16[64,256]{1,0:T(8,128)(2,1)S(1)}, bf16[64,256]{1,0:T(8,128)(2,1)S(1)}, u32[]{:S(2)}, u32[]{:S(2)}) collective-permute-start(bf16[64,256]{1,0:T(8,128)(2,1)S(1)} %collective-permute-done.9), channel_id=1, source_target_pairs={{4,0},{8,4},{12,8},{16,12},{20,16},{24,20},{28,24},{0,28},{5,1},{9... | collective-permute-start | bytes 98312 | tf_op jit(solution)/shard_map/ppermute | solution.py:107
  88.7 6.7 %collective-permute-start.7 = (bf16[64,256]{1,0:T(8,128)(2,1)S(1)}, bf16[64,256]{1,0:T(8,128)(2,1)S(1)}, u32[]{:S(2)}, u32[]{:S(2)}) collective-permute-start(bf16[64,256]{1,0:T(8,128)(2,1)S(1)} %collective-permute-done.6), channel_id=1, source_target_pairs={{0,4},{4,8},{8,12},{12,16},{16,20},{20,24},{24,28},{28,0},{1,5},{5... | collective-permute-start | bytes 98312 | tf_op jit(solution)/shard_map/ppermute | solution.py:102
  100.3 15.9 %all-to-all-start = ((bf16[64,4,1536]{2,0,1:T(8,128)(2,1)}), bf16[64,4,1536]{2,0,1:T(8,128)(2,1)}, u32[]{:S(2)}, u32[]{:S(2)}) async-start(bf16[64,4,1536]{2,0,1:T(8,128)(2,1)} %bitcast.160), calls=%async_computation | async-start | bytes 1572864 | tf_op jit(solution)/shard_map/all_to_all | solution.py:70
  104.5 151.6 %all-gather.2.cloned.1.call-start = ((), (), s32[]{:S(2)}) async-start(), calls=%async_computation.7 | async-start | bytes 2359296 | tf_op jit(solution)/shard_map/all_gather | solution.py:205
  120.9 2.6 copy-start.6
  120.9 3.6 %copy-start.8 = (bf16[6,2,256,128]{3,2,1,0:T(8,128)(2,1)}, bf16[6,2,256,128]{3,2,1,0:T(8,128)(2,1)S(1)}, u32[]{:S(2)}) copy-start(bf16[6,2,256,128]{3,2,1,0:T(8,128)(2,1)S(1)} %get-tuple-element.236) | copy-start | bytes 2359300 | tf_op jit(solution)/shard_map/while
  126.9 2.1 copy-start.2
  129.0 3.0 %copy-start.5 = (pred[256,1792]{1,0:T(8,128)(4,1)S(1)}, pred[256,1792]{1,0:T(8,128)(4,1)}, u32[]{:S(2)}) copy-start(pred[256,1792]{1,0:T(8,128)(4,1)} %copy-done.4) | copy-start | bytes 1376260 | tf_op jit(solution)/shard_map/while
  129.0 3.0 %copy-start.7 = (bf16[1792,128]{1,0:T(8,128)(2,1)S(1)}, bf16[1792,128]{1,0:T(8,128)(2,1)}, u32[]{:S(2)}) copy-start(bf16[1792,128]{1,0:T(8,128)(2,1)} %copy-done.6) | copy-start | bytes 1376260 | tf_op jit(solution)/shard_map/while
  129.0 2.9 %copy-start.9 = (bf16[6,2,256,128]{3,2,1,0:T(8,128)(2,1)S(1)}, bf16[6,2,256,128]{3,2,1,0:T(8,128)(2,1)}, u32[]{:S(2)}) copy-start(bf16[6,2,256,128]{3,2,1,0:T(8,128)(2,1)} %copy-done.8) | copy-start | bytes 2359300 | tf_op jit(solution)/shard_map/while
  131.9 2.7 copy-start.6
  132.0 3.6 %copy-start.8 = (bf16[6,2,256,128]{3,2,1,0:T(8,128)(2,1)}, bf16[6,2,256,128]{3,2,1,0:T(8,128)(2,1)S(1)}, u32[]{:S(2)}) copy-start(bf16[6,2,256,128]{3,2,1,0:T(8,128)(2,1)S(1)} %get-tuple-element.236) | copy-start | bytes 2359300 | tf_op jit(solution)/shard_map/while
  137.9 2.1 copy-start.2
  140.0 3.3 %copy-start.5 = (pred[256,1792]{1,0:T(8,128)(4,1)S(1)}, pred[256,1792]{1,0:T(8,128)(4,1)}, u32[]{:S(2)}) copy-start(pred[256,1792]{1,0:T(8,128)(4,1)} %copy-done.4) | copy-start | bytes 1376260 | tf_op jit(solution)/shard_map/while
  140.0 3.3 %copy-start.7 = (bf16[1792,128]{1,0:T(8,128)(2,1)S(1)}, bf16[1792,128]{1,0:T(8,128)(2,1)}, u32[]{:S(2)}) copy-start(bf16[1792,128]{1,0:T(8,128)(2,1)} %copy-done.6) | copy-start | bytes 1376260 | tf_op jit(solution)/shard_map/while
  140.0 3.3 %copy-start.9 = (bf16[6,2,256,128]{3,2,1,0:T(8,128)(2,1)S(1)}, bf16[6,2,256,128]{3,2,1,0:T(8,128)(2,1)}, u32[]{:S(2)}) copy-start(bf16[6,2,256,128]{3,2,1,0:T(8,128)(2,1)} %copy-done.8) | copy-start | bytes 2359300 | tf_op jit(solution)/shard_map/while
  143.3 2.7 copy-start.6
  143.3 3.6 %copy-start.8 = (bf16[6,2,256,128]{3,2,1,0:T(8,128)(2,1)}, bf16[6,2,256,128]{3,2,1,0:T(8,128)(2,1)S(1)}, u32[]{:S(2)}) copy-start(bf16[6,2,256,128]{3,2,1,0:T(8,128)(2,1)S(1)} %get-tuple-element.236) | copy-start | bytes 2359300 | tf_op jit(solution)/shard_map/while
  149.3 2.1 copy-start.2
  151.4 3.3 %copy-start.5 = (pred[256,1792]{1,0:T(8,128)(4,1)S(1)}, pred[256,1792]{1,0:T(8,128)(4,1)}, u32[]{:S(2)}) copy-start(pred[256,1792]{1,0:T(8,128)(4,1)} %copy-done.4) | copy-start | bytes 1376260 | tf_op jit(solution)/shard_map/while
  151.4 3.3 %copy-start.7 = (bf16[1792,128]{1,0:T(8,128)(2,1)S(1)}, bf16[1792,128]{1,0:T(8,128)(2,1)}, u32[]{:S(2)}) copy-start(bf16[1792,128]{1,0:T(8,128)(2,1)} %copy-done.6) | copy-start | bytes 1376260 | tf_op jit(solution)/shard_map/while
  151.4 3.3 %copy-start.9 = (bf16[6,2,256,128]{3,2,1,0:T(8,128)(2,1)S(1)}, bf16[6,2,256,128]{3,2,1,0:T(8,128)(2,1)}, u32[]{:S(2)}) copy-start(bf16[6,2,256,128]{3,2,1,0:T(8,128)(2,1)} %copy-done.8) | copy-start | bytes 2359300 | tf_op jit(solution)/shard_map/while
  154.7 2.0 copy-start.4
  154.7 2.7 copy-start.6
  154.7 3.6 %copy-start.8 = (bf16[6,2,256,128]{3,2,1,0:T(8,128)(2,1)}, bf16[6,2,256,128]{3,2,1,0:T(8,128)(2,1)S(1)}, u32[]{:S(2)}) copy-start(bf16[6,2,256,128]{3,2,1,0:T(8,128)(2,1)S(1)} %get-tuple-element.236) | copy-start | bytes 2359300 | tf_op jit(solution)/shard_map/while
  160.7 2.1 copy-start.2
  162.8 3.3 %copy-start.5 = (pred[256,1792]{1,0:T(8,128)(4,1)S(1)}, pred[256,1792]{1,0:T(8,128)(4,1)}, u32[]{:S(2)}) copy-start(pred[256,1792]{1,0:T(8,128)(4,1)} %copy-done.4) | copy-start | bytes 1376260 | tf_op jit(solution)/shard_map/while
  162.8 3.3 %copy-start.7 = (bf16[1792,128]{1,0:T(8,128)(2,1)S(1)}, bf16[1792,128]{1,0:T(8,128)(2,1)}, u32[]{:S(2)}) copy-start(bf16[1792,128]{1,0:T(8,128)(2,1)} %copy-done.6) | copy-start | bytes 1376260 | tf_op jit(solution)/shard_map/while
  162.8 3.3 %copy-start.9 = (bf16[6,2,256,128]{3,2,1,0:T(8,128)(2,1)S(1)}, bf16[6,2,256,128]{3,2,1,0:T(8,128)(2,1)}, u32[]{:S(2)}) copy-start(bf16[6,2,256,128]{3,2,1,0:T(8,128)(2,1)} %copy-done.8) | copy-start | bytes 2359300 | tf_op jit(solution)/shard_map/while
  166.1 2.0 copy-start.4
  166.1 2.7 copy-start.6
  166.1 3.6 %copy-start.8 = (bf16[6,2,256,128]{3,2,1,0:T(8,128)(2,1)}, bf16[6,2,256,128]{3,2,1,0:T(8,128)(2,1)S(1)}, u32[]{:S(2)}) copy-start(bf16[6,2,256,128]{3,2,1,0:T(8,128)(2,1)S(1)} %get-tuple-element.236) | copy-start | bytes 2359300 | tf_op jit(solution)/shard_map/while
  172.1 2.1 copy-start.2
  174.2 3.3 %copy-start.5 = (pred[256,1792]{1,0:T(8,128)(4,1)S(1)}, pred[256,1792]{1,0:T(8,128)(4,1)}, u32[]{:S(2)}) copy-start(pred[256,1792]{1,0:T(8,128)(4,1)} %copy-done.4) | copy-start | bytes 1376260 | tf_op jit(solution)/shard_map/while
  174.2 3.3 %copy-start.7 = (bf16[1792,128]{1,0:T(8,128)(2,1)S(1)}, bf16[1792,128]{1,0:T(8,128)(2,1)}, u32[]{:S(2)}) copy-start(bf16[1792,128]{1,0:T(8,128)(2,1)} %copy-done.6) | copy-start | bytes 1376260 | tf_op jit(solution)/shard_map/while
  174.2 3.3 %copy-start.9 = (bf16[6,2,256,128]{3,2,1,0:T(8,128)(2,1)S(1)}, bf16[6,2,256,128]{3,2,1,0:T(8,128)(2,1)}, u32[]{:S(2)}) copy-start(bf16[6,2,256,128]{3,2,1,0:T(8,128)(2,1)} %copy-done.8) | copy-start | bytes 2359300 | tf_op jit(solution)/shard_map/while
  177.5 2.0 copy-start.4
  177.5 2.7 copy-start.6
  177.5 3.6 %copy-start.8 = (bf16[6,2,256,128]{3,2,1,0:T(8,128)(2,1)}, bf16[6,2,256,128]{3,2,1,0:T(8,128)(2,1)S(1)}, u32[]{:S(2)}) copy-start(bf16[6,2,256,128]{3,2,1,0:T(8,128)(2,1)S(1)} %get-tuple-element.236) | copy-start | bytes 2359300 | tf_op jit(solution)/shard_map/while
  183.5 2.1 copy-start.2
  185.6 3.3 %copy-start.5 = (pred[256,1792]{1,0:T(8,128)(4,1)S(1)}, pred[256,1792]{1,0:T(8,128)(4,1)}, u32[]{:S(2)}) copy-start(pred[256,1792]{1,0:T(8,128)(4,1)} %copy-done.4) | copy-start | bytes 1376260 | tf_op jit(solution)/shard_map/while
  185.6 3.3 %copy-start.7 = (bf16[1792,128]{1,0:T(8,128)(2,1)S(1)}, bf16[1792,128]{1,0:T(8,128)(2,1)}, u32[]{:S(2)}) copy-start(bf16[1792,128]{1,0:T(8,128)(2,1)} %copy-done.6) | copy-start | bytes 1376260 | tf_op jit(solution)/shard_map/while
  185.6 3.3 %copy-start.9 = (bf16[6,2,256,128]{3,2,1,0:T(8,128)(2,1)S(1)}, bf16[6,2,256,128]{3,2,1,0:T(8,128)(2,1)}, u32[]{:S(2)}) copy-start(bf16[6,2,256,128]{3,2,1,0:T(8,128)(2,1)} %copy-done.8) | copy-start | bytes 2359300 | tf_op jit(solution)/shard_map/while
  190.1 7.2 %copy-start.10 = (f32[1792,256]{1,0:T(8,128)}, f32[1792,256]{1,0:T(8,128)S(1)}, u32[]{:S(2)}) copy-start(f32[1792,256]{1,0:T(8,128)S(1)} %constant_dynamic-update-slice_fusion.21) | copy-start | bytes 5505028
  192.0 62.9 %collective-permute-start.11 = (f32[256,256]{1,0:T(8,128)}, f32[256,256]{1,0:T(8,128)S(1)}, u32[]{:S(2)}, u32[]{:S(2)}) collective-permute-start(f32[256,256]{1,0:T(8,128)} %get-tuple-element.124), channel_id=1, source_target_pairs={{4,0},{8,4},{12,8},{16,12},{20,16},{24,20},{28,24},{5,1},{9,5},{13... | collective-permute-start | bytes 786440 | tf_op jit(solution)/shard_map/ppermute | solution.py:22
  193.2 61.6 %collective-permute-start.12 = (f32[256,256]{1,0:T(8,128)}, f32[256,256]{1,0:T(8,128)S(1)}, u32[]{:S(2)}, u32[]{:S(2)}) collective-permute-start(f32[256,256]{1,0:T(8,128)} %get-tuple-element.127), channel_id=1, source_target_pairs={{8,0},{12,4},{16,8},{20,12},{24,16},{28,20},{9,1},{13,5},{17,9},{2... | collective-permute-start | bytes 786440 | tf_op jit(solution)/shard_map/ppermute | solution.py:22
  194.5 60.3 %collective-permute-start.13 = (f32[256,256]{1,0:T(8,128)}, f32[256,256]{1,0:T(8,128)}, u32[]{:S(2)}, u32[]{:S(2)}) collective-permute-start(f32[256,256]{1,0:T(8,128)} %get-tuple-element.126), channel_id=1, source_target_pairs={{12,0},{16,4},{20,8},{24,12},{28,16},{13,1},{17,5},{21,9},{25,13},... | collective-permute-start | bytes 786440 | tf_op jit(solution)/shard_map/ppermute | solution.py:22
  195.8 59.0 %collective-permute-start.14 = (f32[256,256]{1,0:T(8,128)}, f32[256,256]{1,0:T(8,128)}, u32[]{:S(2)}, u32[]{:S(2)}) collective-permute-start(f32[256,256]{1,0:T(8,128)} %get-tuple-element.125), channel_id=1, source_target_pairs={{16,0},{20,4},{24,8},{28,12},{17,1},{21,5},{25,9},{29,13},{18,2},{... | collective-permute-start | bytes 786440 | tf_op jit(solution)/shard_map/ppermute | solution.py:22
  201.1 59.2 %all-to-all-start.4 = ((f32[4,64,1536]{2,1,0:T(8,128)}), f32[4,64,1536]{2,1,0:T(8,128)S(1)}, u32[]{:S(2)}, u32[]{:S(2)}) async-start(f32[4,64,1536]{2,1,0:T(8,128)} %all_to_all.108), calls=%async_computation.4 | async-start | bytes 3145728 | tf_op jit(solution)/shard_map/all_to_all | solution.py:212
  260.2 7.9 %all-to-all-start.6 = ((f32[4,64,128]{2,1,0:T(8,128)}), f32[4,64,128]{2,1,0:T(8,128)S(1)}, u32[]{:S(2)}, u32[]{:S(2)}) async-start(f32[4,64,128]{2,1,0:T(8,128)} %bitcast.39), calls=%async_computation.6 | async-start | bytes 262144 | tf_op jit(solution)/shard_map/all_to_all | solution.py:214
  268.1 7.9 %all-to-all-start.5 = ((f32[4,64,128]{2,1,0:T(8,128)}), f32[4,64,128]{2,1,0:T(8,128)S(1)}, u32[]{:S(2)}, u32[]{:S(2)}) async-start(f32[4,64,128]{2,1,0:T(8,128)} %bitcast.37), calls=%async_computation.5 | async-start | bytes 262144 | tf_op jit(solution)/shard_map/all_to_all | solution.py:213
  (11 other events, 18.7 us)
Sparse Core Ops, SparseCore 0:
  191.1 64.2 all-gather.1
